TPU v7x, 128 devices: a whole 4x4x4 slice. The times are simulated.
128 devices in a mesh: dom: 16 (over x, y), cls: 8 (over z, core).
Axes of the slice: x: 4, y: 4, z: 4, core: 2. Of those that a mesh axis runs over, the one named last changes fastest.
Arguments:
- stack: bfloat16 [32768, 2, 64, 128], P(('dom', 'cls')), may hold values from -6 to 6
- batch_index: int32 [16384], P(('dom', 'cls')), may hold values from 0 to 255, as said below
- best_class: int32 [16384], P(('dom', 'cls')), may hold values from 0 to 511, as said below
- best_rot: int32 [16384], P(('dom', 'cls')), may hold values from 0 to 63
- best_shift: int32 [16384, 2], P(('dom', 'cls')), may hold values from -4 to 4
- ctf: bfloat16 [16384, 64], P(('dom', 'cls')), may hold values from -1 to 1
- averages: float32 [512, 2, 64, 128], P(('dom', 'cls')), may hold values from -6 to 6
- velocity: float32 [512, 2, 64, 128], P(('dom', 'cls')), may hold values from -3 to 3
Outputs:
- new_averages: float32 [512, 2, 64, 128], P(('dom', 'cls'))
- new_velocity: float32 [512, 2, 64, 128], P(('dom', 'cls'))
- errors: float32 [16384], P(('dom', 'cls'))
Inputs may be any that keep to these rules, and one draw needn't show every extreme that they name: `batch_index`: each aligned block of 128 entries (one device's particles) holds distinct row numbers into that device's own 256 rows of stack. `best_class`: classes c with equal c // 32 form a group. In each aligned block of 128 entries (one device's particles) at most 16 entries name classes of one group, and some group is named by exactly 16 entries of that block.
All inputs are finite; a program needn't handle non-finite values.
Results may differ from a plain program's by a relative error of at most 0.0026.
Values may be sent and summed in bfloat16 or wider, within the bound.
No kernel may reach another device: no remote copies, remote signals or barrier semaphores. Data moves between devices by JAX's collectives and lax.ppermute only.
A program may use at most 128 MiB of HBM per device.

v0:
```python
import jax
import jax.numpy as jnp
from jax import lax
from jax.sharding import PartitionSpec as P

IMG = 128
TWO_PI = 6.283185307179586
MOMENTUM = 0.9
RATE = 0.5
RIDGE = 1.0


def align_rows(rows, rotation, shift):
    cycles = rows.shape[2]
    angles = rows.shape[3]
    radius = jnp.arange(cycles).astype(jnp.float32) + 1.0
    theta = TWO_PI * jnp.arange(angles).astype(jnp.float32) / angles
    shift_x = shift[:, 0].astype(jnp.float32)
    shift_y = shift[:, 1].astype(jnp.float32)
    along = (
        jnp.cos(theta)[None, None, :] * shift_x[:, None, None]
        + jnp.sin(theta)[None, None, :] * shift_y[:, None, None]
    )
    phase = TWO_PI * radius[None, :, None] * along / IMG
    cosine = jnp.cos(phase)
    sine = jnp.sin(phase)
    real = rows[:, 0].astype(jnp.float32)
    imag = rows[:, 1].astype(jnp.float32)
    turned = jnp.stack([cosine * real - sine * imag, sine * real + cosine * imag], axis=1).astype(
        jnp.bfloat16
    )
    source = (jnp.arange(angles)[None, :] + 2 * rotation[:, None]) % angles
    permute = (source[:, :, None] == jnp.arange(angles)[None, None, :]).astype(jnp.bfloat16)
    moved = jnp.einsum("pskb,pab->pska", turned, permute, preferred_element_type=jnp.float32)
    return moved.astype(jnp.bfloat16)


def class_table(marker, column):
    local = marker.astype(jnp.int32) - 1
    return (jnp.arange(column)[:, None] == local[None, :]).astype(jnp.bfloat16)


def class_partials(table, terms, gamma):
    grads = jnp.dot(table, terms, preferred_element_type=jnp.float32)
    gamma_float = gamma.astype(jnp.float32)
    weights = jnp.dot(
        table.astype(jnp.float32),
        gamma_float * gamma_float,
        precision=lax.Precision.HIGHEST,
        preferred_element_type=jnp.float32,
    )
    return (grads, weights)


def on_device(stack, batch_index, best_class, best_rot, best_shift, ctf, averages, velocity):
    count = batch_index.shape[0]
    cycles = ctf.shape[1]
    angles = stack.shape[3]
    stored = stack.shape[0]
    flat = 2 * cycles * angles
    owners = lax.axis_size("dom")
    column = lax.axis_size("cls") * averages.shape[0]
    slots = 2 * count // owners
    buffer_rows = owners * slots
    picker = (batch_index[:, None] == jnp.arange(stored)[None, :]).astype(jnp.bfloat16)
    rows = jnp.dot(picker, stack.reshape(stored, flat), preferred_element_type=jnp.float32)
    rows = rows.astype(jnp.bfloat16).reshape(count, 2, cycles, angles)
    aligned = align_rows(rows, best_rot, best_shift)
    owner = best_class // column
    local_class = best_class - owner * column
    placed = (owner[:, None] == jnp.arange(owners)[None, :]).astype(jnp.int32)
    position = jnp.sum(jnp.cumsum(placed, axis=0) * placed, axis=1) - 1
    target = owner * slots + position
    dispatch = (jnp.arange(buffer_rows)[:, None] == target[None, :]).astype(jnp.bfloat16)

    def pack(payload):
        packed = jnp.dot(dispatch, payload, preferred_element_type=jnp.float32).astype(jnp.bfloat16)
        return packed.reshape(owners, slots, payload.shape[1])

    ctf_packed = pack(ctf)
    marker_packed = pack((local_class + 1).astype(jnp.bfloat16)[:, None]).reshape(owners, slots)
    every = lax.all_gather(averages.astype(jnp.bfloat16), ("dom", "cls"), axis=0, tiled=True)
    total_classes = every.shape[0]
    chooser = (best_class[:, None] == jnp.arange(total_classes)[None, :]).astype(jnp.bfloat16)
    model = jnp.dot(
        chooser, every.reshape(total_classes, flat), preferred_element_type=jnp.float32
    ).reshape(count, 2, cycles, angles)
    gamma_wide = ctf.astype(jnp.float32)[:, None, :, None]
    resid = aligned.astype(jnp.float32) - gamma_wide * model
    errors = jnp.mean(resid * resid, axis=(1, 2, 3))
    term = (gamma_wide * resid).astype(jnp.bfloat16).reshape(count, flat)
    arrived = (
        lax.all_to_all(pack(term), "dom", split_axis=0, concat_axis=0, tiled=True),
        lax.all_to_all(ctf_packed, "dom", split_axis=0, concat_axis=0, tiled=True),
        lax.all_to_all(marker_packed, "dom", split_axis=0, concat_axis=0, tiled=True),
    )
    got_terms = arrived[0].reshape(buffer_rows, flat)
    got_gamma = arrived[1].reshape(buffer_rows, cycles)
    table = class_table(arrived[2].reshape(buffer_rows), column)
    grads, weights = class_partials(table, got_terms, got_gamma)
    summed, weight_sum = (
        lax.psum_scatter(grads, "cls", scatter_dimension=0, tiled=True),
        lax.psum_scatter(weights, "cls", scatter_dimension=0, tiled=True),
    )
    step = (summed.reshape(averages.shape) - RIDGE * averages) / (
        weight_sum[:, None, :, None] + RIDGE
    )
    new_velocity = MOMENTUM * velocity + step
    new_averages = averages + RATE * new_velocity
    return (new_averages, new_velocity, errors)


def solution(mesh):
    in_specs = (
        P(("dom", "cls"), None, None, None),
        P(("dom", "cls")),
        P(("dom", "cls")),
        P(("dom", "cls")),
        P(("dom", "cls"), None),
        P(("dom", "cls"), None),
        P(("dom", "cls"), None, None, None),
        P(("dom", "cls"), None, None, None),
    )
    out_specs = (
        P(("dom", "cls"), None, None, None),
        P(("dom", "cls"), None, None, None),
        P(("dom", "cls")),
    )
    return jax.shard_map(
        on_device, mesh=mesh, in_specs=in_specs, out_specs=out_specs, check_vma=False
    )
```

profile of v0, /device:TPU:0, one launch (start us, length us, event | category | flops | bytes accessed | tf_op | source)
XLA Modules:
  0.0 396.0 jit_solution(6878493428379385242)
XLA Ops:
  7.2 0.0 all-gather.2.cloned.1.call-start
  7.2 1.6 convert_element_type.118
  8.8 0.0 all-gather.2.cloned.1.call-update
  8.9 0.7 and_select_fusion
  9.5 0.1 fusion.38
  9.6 0.2 reduce_window_sum.11
  9.8 0.2 select_reduce_fusion
  10.0 0.7 add_add_fusion
  10.6 0.8 fusion.30
  11.4 0.7 all_to_all.16
  12.2 7.1 %all-to-all-start = ((bf16[16,1,16]{2,1,0:T(2,128)(2,1)}), bf16[16,1,16]{2,1,0:T(2,128)(2,1)S(1)}, u32[]{:S(2)}, u32[]{:S(2)}) async-start(bf16[16,1,16]{2,1,0:T(2,128)(2,1)} %all_to_all.16), calls=%async_computation | async-start | bytes 16384 | tf_op jit(solution)/shard_map/all_to_all | solution.py:95
  19.3 0.8 copy.19
  20.1 8.8 %fusion.24 = bf16[16,8,128,128]{3,1,2,0:T(8,128)(2,1)S(1)} fusion(bf16[32,8,128,128]{3,2,1,0:T(8,128)(2,1)} %bitcast.59, s32[128]{0:T(128)} %param.9), kind=kOutput, calls=%fused_computation.30 | convolution fusion | flops 1075871744 | bytes 12583424 | tf_op jit(solution)/shard_map/dot_general | solution.py:66
  28.9 0.0 copy-start.5
  28.9 0.0 copy-start.3
  28.9 1.2 copy.27
  30.3 0.0 copy-done.5
  30.3 0.0 copy-done.3
  30.3 0.1 add_select_fusion
  30.4 0.1 multiply_add_fusion.1
  30.5 17.4 %fusion.8 = (bf16[128,1,64,128]{3,2,1,0:T(8,128)(2,1)S(1)}, bf16[128,1,64,128]{3,2,1,0:T(8,128)(2,1)}) fusion(f32[128,128]{1,0:T(8,128)S(1)} %multiply_add_fusion.1, f32[64]{0:T(128)S(1)} %add_multiply_fusion, bf16[128,2,64,128]{3,2,1,0:T(8,128)(2,1)S(1)} %bitcast.58), kind=kLoop, calls=%fused_computation.17 | loop fusion | flops 12582912 | bytes 8454400 | tf_op jit(solution)/shard_map/convert
  47.9 46.7 %all-gather.2.cloned.1.call-done = bf16[512,2,64,128]{3,2,1,0:T(8,128)(2,1)} async-done(((bf16[4,2,64,128]{3,2,1,0:T(8,128)(2,1)}), bf16[512,2,64,128]{3,2,1,0:T(8,128)(2,1)}) %all-gather.2.cloned.1.call-update) | async-done | bytes 16777232 | tf_op jit(solution)/shard_map/all_gather | solution.py:82
  94.6 23.9 %copy.25 = bf16[512,2,64,128]{0,3,2,1:T(8,128)(2,1)} copy(bf16[512,2,64,128]{3,2,1,0:T(8,128)(2,1)} %all-gather.2.cloned.1.call-done) | data formatting | bytes 33554432 | tf_op jit(solution)/shard_map/reshape | solution.py:86
  118.5 0.0 copy-done.4
  118.5 13.6 %fusion = f32[128,2,64,128]{0,3,2,1:T(8,128)} fusion(bf16[512,2,64,128]{0,3,2,1:T(8,128)(2,1)} %copy.25, s32[128]{0:T(128)S(1)} %copy-done.4), kind=kOutput, calls=%fused_computation.2 | convolution fusion | flops 2147549184 | bytes 25166336 | tf_op jit(solution)/shard_map/dot_general | solution.py:85
  132.1 8.7 %copy.21 = f32[128,2,64,128]{3,2,1,0:T(8,128)} copy(f32[128,2,64,128]{0,3,2,1:T(8,128)} %fusion) | data formatting | bytes 16777216 | tf_op jit(solution)/shard_map/dot_general | solution.py:85
  140.8 9.4 %multiply_reduce_fusion = (f32[128]{0:T(128)S(1)}, bf16[128,2,64,128]{3,2,1,0:T(8,128)(2,1)S(1)}) fusion(f32[128,2,64,128]{3,2,1,0:T(8,128)} %copy.21, f32[128,64]{1,0:T(8,128)S(1)} %copy.19, s32[128,128]{1,0:T(8,128)S(1)} %add_select_fusion, bf16[128,1,64,128]{3,2,1,0:T(8,128)(2,1)} %get-tuple-element.8, bf16[128,1,64,128]{3,2,1,0:T(8,128)(2,1)S(1)} %get-tuple-element.7), kind=kOutput, calls=%fused_computation.6 | convolution fusion | flops 557842304 | bytes 16876032 | tf_op jit(solution)/shard_map/pskb,pab->pska/dot_general | solution.py:34
  150.2 6.7 %convolution_convert_fusion = bf16[256,16384]{1,0:T(8,128)(2,1)} fusion(bf16[16,8,128,128]{3,2,1,0:T(8,128)(2,1)S(1)} %bitcast.60, s32[128]{0:T(128)S(1)} %add_add_fusion), kind=kOutput, calls=%fused_computation | convolution fusion | flops 1077968896 | bytes 12583424 | tf_op jit(solution)/shard_map/dot_general | solution.py:77
  156.9 0.0 all-to-all-done
  156.9 6.9 %all-to-all-start.1 = ((bf16[16,16,16384]{2,1,0:T(8,128)(2,1)}), bf16[16,16,16384]{2,1,0:T(8,128)(2,1)}, u32[]{:S(2)}, u32[]{:S(2)}) async-start(bf16[16,16,16384]{2,1,0:T(8,128)(2,1)} %bitcast.57), calls=%async_computation.1 | async-start | bytes 16777216 | tf_op jit(solution)/shard_map/all_to_all | solution.py:93
  163.8 0.0 all-reduce.4.cloned.1.call-start
  163.9 0.1 sub.32
  163.9 146.1 %all-to-all-done.1 = bf16[16,16,16384]{2,1,0:T(8,128)(2,1)} async-done(((bf16[16,16,16384]{2,1,0:T(8,128)(2,1)}), bf16[16,16,16384]{2,1,0:T(8,128)(2,1)}, u32[]{:S(2)}, u32[]{:S(2)}) %all-to-all-start.1) | async-done | bytes 8388640 | tf_op jit(solution)/shard_map/all_to_all | solution.py:93
  310.0 6.3 %fusion.41 = f32[32,16384]{1,0:T(8,128)} fusion(bf16[256,16384]{1,0:T(8,128)(2,1)} %bitcast.12, s32[256]{0:T(256)S(1)} %sub.32), kind=kOutput, calls=%fused_computation.59 | convolution fusion | flops 268443648 | bytes 10486784 | tf_op jit(solution)/shard_map/dot_general | solution.py:44
  316.3 0.0 all-reduce.4.cloned.1.call-update
  316.4 0.1 convolution_convert_fusion.2
  316.5 0.1 copy.22
  316.7 0.7 reshape.217
  317.4 11.7 %all-to-all-start.2 = ((bf16[16,2,512]{2,1,0:T(2,128)(2,1)}), bf16[16,2,512]{2,1,0:T(2,128)(2,1)S(1)}, u32[]{:S(2)}, u32[]{:S(2)}) async-start(bf16[16,2,512]{2,1,0:T(2,128)(2,1)} %reshape.217), calls=%async_computation.2 | async-start | bytes 65536 | tf_op jit(solution)/shard_map/all_to_all | solution.py:94
  329.1 0.6 dynamic-slice
  330.3 6.4 %all-to-all-done.2 = bf16[16,2,512]{2,1,0:T(2,128)(2,1)S(1)} async-done(((bf16[16,2,512]{2,1,0:T(2,128)(2,1)}), bf16[16,2,512]{2,1,0:T(2,128)(2,1)S(1)}, u32[]{:S(2)}, u32[]{:S(2)}) %all-to-all-start.2) | async-done | bytes 32800 | tf_op jit(solution)/shard_map/all_to_all | solution.py:94
  336.7 0.1 reshape.218
  336.8 0.2 fusion.40
  337.0 23.6 %all-reduce.1 = f32[32,64]{1,0:T(8,128)S(1)} all-reduce(f32[32,64]{1,0:T(8,128)S(1)} %fusion.40), channel_id=3, replica_groups=mesh['dom'=16,'cls'=8] {'cls'}, use_global_device_ids=true, to_apply=%region_3.4.clone | all-reduce | flops 2048 | bytes 16384
  360.6 0.5 broadcast_multiply_fusion
  361.1 26.0 %all-reduce.4.cloned.1.call-done = f32[32,16384]{1,0:T(8,128)} async-done(((f32[32,16384]{1,0:T(8,128)}), f32[32,16384]{1,0:T(8,128)}) %all-reduce.4.cloned.1.call-update) | async-done | bytes 2097168
  387.0 1.1 dynamic-slice_bitcast_fusion
  388.2 1.0 multiply_add_fusion
  (18 shorter events, 0.2 us)
Async XLA Ops:
  7.2 87.4 %all-gather.2.cloned.1.call-start = ((), (), s32[]{:S(2)}) async-start(), calls=%async_computation.3 | async-start | bytes 16908288 | tf_op jit(solution)/shard_map/all_gather | solution.py:82
  12.2 144.8 %all-to-all-start = ((bf16[16,1,16]{2,1,0:T(2,128)(2,1)}), bf16[16,1,16]{2,1,0:T(2,128)(2,1)S(1)}, u32[]{:S(2)}, u32[]{:S(2)}) async-start(bf16[16,1,16]{2,1,0:T(2,128)(2,1)} %all_to_all.16), calls=%async_computation | async-start | bytes 16384 | tf_op jit(solution)/shard_map/all_to_all | solution.py:95
  28.9 1.3 copy-start.5
  28.9 1.3 copy-start.3
  47.9 70.6 %copy-start.4 = (s32[128]{0:T(128)S(1)}, s32[128]{0:T(128)}, u32[]{:S(2)}) copy-start(s32[128]{0:T(128)} %param.10) | copy-start | bytes 1540
  156.9 153.1 %all-to-all-start.1 = ((bf16[16,16,16384]{2,1,0:T(8,128)(2,1)}), bf16[16,16,16384]{2,1,0:T(8,128)(2,1)}, u32[]{:S(2)}, u32[]{:S(2)}) async-start(bf16[16,16,16384]{2,1,0:T(8,128)(2,1)} %bitcast.57), calls=%async_computation.1 | async-start | bytes 16777216 | tf_op jit(solution)/shard_map/all_to_all | solution.py:93
  163.8 223.3 %all-reduce.4.cloned.1.call-start = ((), (), s32[]{:S(2)}) async-start(), calls=%async_computation.4 | async-start | bytes 4194304
  310.0 6.3 %copy-start.2 = (bf16[128,64]{0,1:T(8,128)(2,1)S(1)}, bf16[128,64]{0,1:T(8,128)(2,1)}, u32[]{:S(2)}) copy-start(bf16[128,64]{0,1:T(8,128)(2,1)} %param.13) | copy-start | bytes 49156
  310.0 19.1 %copy-start.6 = (u32[128]{0:T(128)S(1)}, u32[128]{0:T(128)}, u32[]{:S(2)}) copy-start(u32[128]{0:T(128)} %constant.71) | copy-start | bytes 1540
  310.0 78.1 %copy-start = (f32[4,2,64,128]{3,2,1,0:T(8,128)S(1)}, f32[4,2,64,128]{3,2,1,0:T(8,128)}, u32[]{:S(2)}) copy-start(f32[4,2,64,128]{3,2,1,0:T(8,128)} %param.14) | copy-start | bytes 786436
  310.0 78.1 %copy-start.1 = (f32[4,2,64,128]{3,2,1,0:T(8,128)S(1)}, f32[4,2,64,128]{3,2,1,0:T(8,128)}, u32[]{:S(2)}) copy-start(f32[4,2,64,128]{3,2,1,0:T(8,128)} %param.15) | copy-start | bytes 786436
  317.4 19.3 %all-to-all-start.2 = ((bf16[16,2,512]{2,1,0:T(2,128)(2,1)}), bf16[16,2,512]{2,1,0:T(2,128)(2,1)S(1)}, u32[]{:S(2)}, u32[]{:S(2)}) async-start(bf16[16,2,512]{2,1,0:T(2,128)(2,1)} %reshape.217), calls=%async_computation.2 | async-start | bytes 65536 | tf_op jit(solution)/shard_map/all_to_all | solution.py:94
Sparse Core Ops, SparseCore 0:
  11.7 82.8 all-gather.1
  316.5 70.5 all-reduce.3
where the time goes:
time: 397 us; the launch traced here: 396 us
  waiting for transfers between devices  225 us (57%)
  matrix products  45.9 us (12%)
  local copies, waits for them, and re-layouts  38.1 us (10%)
  starting transfers between devices  25.8 us (6%)
  blocking collectives  23.6 us (6%)
  other arithmetic  22.6 us (6%)
  between operations  14.9 us (4%)
    all_to_all x1, waiting for transfers between devices, on_device(): lax.all_to_all(pack(term), 'dom', split_axis=0, concat_axis=0, tiled=True)  146 us
    all_gather x1, waiting for transfers between devices, on_device(): lax.all_gather(averages.astype(jnp.bfloat16), ('dom', 'cls'), axis=0, til...  46.7 us
    unnamed x3, waiting for transfers between devices  26 us
    reshape x1, local copies, waits for them, and re-layouts, on_device(): every.reshape(total_classes, flat)  23.9 us
    unnamed x1, blocking collectives  23.6 us
    another operation x1, other arithmetic  17.4 us
    dot_general x1, matrix products, on_device(): jnp.dot(chooser, every.reshape(total_classes, flat), preferred_element_ty...  13.6 us
    all_to_all x1, starting transfers between devices, on_device(): lax.all_to_all(ctf_packed, 'dom', split_axis=0, concat_axis=0, tiled=True)  11.7 us
  transfers between devices with their start and end apart: 5, of which 4 were waited for; matrix products, arithmetic and copies ran while one was open for 24% of the time, Pallas kernels for 0%

commit v1 on v0

--- a/solution.py
+++ b/solution.py
@@ -79,7 +79,15 @@
 
     ctf_packed = pack(ctf)
     marker_packed = pack((local_class + 1).astype(jnp.bfloat16)[:, None]).reshape(owners, slots)
-    every = lax.all_gather(averages.astype(jnp.bfloat16), ("dom", "cls"), axis=0, tiled=True)
+    every = jnp.concatenate(
+        lax.all_to_all(
+            jnp.stack([averages.astype(jnp.bfloat16)] * lax.axis_size(("dom", "cls"))),
+            ("dom", "cls"),
+            0,
+            0,
+        ),
+        axis=0,
+    )
     total_classes = every.shape[0]
     chooser = (best_class[:, None] == jnp.arange(total_classes)[None, :]).astype(jnp.bfloat16)
     model = jnp.dot(

time: 397 us -> 590 us (1.49)
  waiting for transfers between devices: 225 us -> 367 us
  local copies, waits for them, and re-layouts: 38.1 us -> 67.5 us
  starting transfers between devices: 25.8 us -> 44.3 us
    all_to_all x0 -> x1, waiting for transfers between devices: none -> 200 us  [on_device(): lax.all_to_all(jnp.stack([averages.astype(jnp.bfloat16)] * lax.axis_size(...]
    all_gather x1 -> x0, waiting for transfers between devices: 46.7 us -> none  [on_device(): lax.all_gather(averages.astype(jnp.bfloat16), ('dom', 'cls'), axis=0, til...]
    another operation x0 -> x2, local copies, waits for them, and re-layouts: none -> 31.6 us  [the longest x1 25.3 us: on_device(): every.reshape(total_classes, flat)]
    reshape x1 -> x0, local copies, waits for them, and re-layouts: 23.9 us -> none  [on_device(): every.reshape(total_classes, flat)]
    dot_general x1 -> x2, local copies, waits for them, and re-layouts: 8.66 us -> 31.1 us  [on_device(): jnp.dot(chooser, every.reshape(total_classes, flat), preferred_element_ty...]
    all_to_all x1, waiting for transfers between devices: 146 us -> 132 us  [on_device(): lax.all_to_all(pack(term), 'dom', split_axis=0, concat_axis=0, tiled=True)]
    all_to_all x0 -> x1, starting transfers between devices: none -> 11.7 us  [on_device(): lax.all_to_all(jnp.stack([averages.astype(jnp.bfloat16)] * lax.axis_size(...]
    all_to_all x1, starting transfers between devices: 7.12 us -> 16.1 us  [on_device(): lax.all_to_all(marker_packed, 'dom', split_axis=0, concat_axis=0, tiled=T...]
  transfers between devices with their start and end apart: 5 -> 5, of which waited for: 4 -> 4; matrix products, arithmetic and copies ran while one was open for 24% -> 20% of each run, Pallas kernels for 0% -> 0%
where the time goes in v1:
time: 590 us; the launch traced here: 588 us
  waiting for transfers between devices  367 us (62%)
  local copies, waits for them, and re-layouts  67.5 us (11%)
  matrix products  45.3 us (8%)
  starting transfers between devices  44.3 us (8%)
  blocking collectives  28.4 us (5%)
  other arithmetic  20.6 us (3%)
  between operations  14.9 us (3%)
    all_to_all x1, waiting for transfers between devices, on_device(): lax.all_to_all(jnp.stack([averages.astype(jnp.bfloat16)] * lax.axis_size(...  200 us
    all_to_all x1, waiting for transfers between devices, on_device(): lax.all_to_all(pack(term), 'dom', split_axis=0, concat_axis=0, tiled=True)  132 us
    dot_general x2, local copies, waits for them, and re-layouts, on_device(): jnp.dot(chooser, every.reshape(total_classes, flat), preferred_element_ty...  31.1 us
    unnamed x1, blocking collectives  28.4 us
    unnamed x2, waiting for transfers between devices  27.6 us
    another operation x1, local copies, waits for them, and re-layouts, on_device(): every.reshape(total_classes, flat)  25.3 us
    another operation x1, other arithmetic  17.4 us
    all_to_all x1, starting transfers between devices, on_device(): lax.all_to_all(marker_packed, 'dom', split_axis=0, concat_axis=0, tiled=T...  16.1 us
  transfers between devices with their start and end apart: 5, of which 4 were waited for; matrix products, arithmetic and copies ran while one was open for 20% of the time, Pallas kernels for 0%

profile of v1, /device:TPU:0, one launch (start us, length us, event | category | flops | bytes accessed | tf_op | source)
XLA Modules:
  0.0 587.8 jit_solution(2880282425286609938)
XLA Ops:
  7.2 1.0 convert_element_type.118
  8.1 6.3 %stack.6 = bf16[128,4,2,64,128]{4,3,2,1,0:T(8,128)(2,1)} broadcast(bf16[4,2,64,128]{3,2,1,0:T(8,128)(2,1)S(1)} %convert_element_type.118), dimensions={1,2,3,4} | broadcast | bytes 16908288 | tf_op jit(solution)/shard_map/stack | solution.py:84
  14.5 11.7 %all-to-all-start.1 = ((bf16[128,4,2,64,128]{4,3,2,1,0:T(8,128)(2,1)}), bf16[128,4,2,64,128]{4,3,2,1,0:T(8,128)(2,1)}, u32[]{:S(2)}, u32[]{:S(2)}) async-start(bf16[128,4,2,64,128]{4,3,2,1,0:T(8,128)(2,1)} %stack.6), calls=%async_computation.1 | async-start | bytes 33554432 | tf_op jit(solution)/shard_map/all_to_all | solution.py:83
  26.1 0.0 copy-done.5
  26.2 0.1 fusion.37
  26.3 0.2 reduce_window_sum.11
  26.4 0.2 select_reduce_fusion
  26.6 0.1 fusion.29
  26.8 0.7 all_to_all.20
  27.5 0.1 copy.19
  27.6 0.0 copy-done.4
  27.6 8.8 %fusion.22 = bf16[16,8,128,128]{3,1,2,0:T(8,128)(2,1)S(1)} fusion(bf16[32,8,128,128]{3,2,1,0:T(8,128)(2,1)} %bitcast.59, s32[128]{0:T(128)S(1)} %copy-done.4), kind=kOutput, calls=%fused_computation.28 | convolution fusion | flops 1075871744 | bytes 12583424 | tf_op jit(solution)/shard_map/dot_general | solution.py:66
  36.4 0.0 copy-start.6
  36.4 0.0 copy-start.3
  36.4 1.2 copy.26
  37.7 0.0 copy-done.6
  37.8 0.1 add_select_fusion
  37.9 0.1 multiply_add_fusion.1
  38.0 17.4 %fusion.6 = (bf16[128,1,64,128]{3,2,1,0:T(8,128)(2,1)S(1)}, bf16[128,1,64,128]{3,2,1,0:T(8,128)(2,1)}) fusion(f32[128,128]{1,0:T(8,128)S(1)} %multiply_add_fusion.1, f32[64]{0:T(128)S(1)} %add_multiply_fusion, bf16[128,2,64,128]{3,2,1,0:T(8,128)(2,1)S(1)} %bitcast.58), kind=kLoop, calls=%fused_computation.15 | loop fusion | flops 12582912 | bytes 8454400 | tf_op jit(solution)/shard_map/convert
  55.4 200.3 %all-to-all-done.1 = bf16[128,4,2,64,128]{4,3,2,1,0:T(8,128)(2,1)} async-done(((bf16[128,4,2,64,128]{4,3,2,1,0:T(8,128)(2,1)}), bf16[128,4,2,64,128]{4,3,2,1,0:T(8,128)(2,1)}, u32[]{:S(2)}, u32[]{:S(2)}) %all-to-all-start.1) | async-done | bytes 16777248 | tf_op jit(solution)/shard_map/all_to_all | solution.py:83
  255.7 16.1 %all-to-all-start = ((bf16[16,1,16]{2,1,0:T(2,128)(2,1)}), bf16[16,1,16]{2,1,0:T(2,128)(2,1)S(1)}, u32[]{:S(2)}, u32[]{:S(2)}) async-start(bf16[16,1,16]{2,1,0:T(2,128)(2,1)} %all_to_all.20), calls=%async_computation | async-start | bytes 16384 | tf_op jit(solution)/shard_map/all_to_all | solution.py:103
  271.8 25.3 %reshape_reshape.4 = bf16[512,16384]{1,0:T(8,128)(2,1)} reshape(bf16[128,4,2,64,128]{4,3,2,1,0:T(8,128)(2,1)} %all-to-all-done.1) | data formatting | bytes 33554432 | tf_op jit(solution)/shard_map/reshape;reshape | solution.py:94
  297.1 22.4 %copy.20 = bf16[16384,512]{1,0:T(8,128)(2,1)} copy(bf16[16384,512]{0,1:T(8,128)(2,1)} %bitcast.56) | data formatting | bytes 33554432 | tf_op jit(solution)/shard_map/dot_general | solution.py:93
  319.5 13.6 %fusion.26 = f32[128,2,64,128]{0,3,2,1:T(8,128)} fusion(bf16[2,64,128,512]{3,2,1,0:T(8,128)(2,1)} %bitcast.55, s32[128]{0:T(128)S(1)} %copy-done.5), kind=kOutput, calls=%fused_computation.35 | convolution fusion | flops 2147549184 | bytes 25166336 | tf_op jit(solution)/shard_map/dot_general | solution.py:93
  333.1 8.7 %copy.21 = f32[128,2,64,128]{3,2,1,0:T(8,128)} copy(f32[128,2,64,128]{0,3,2,1:T(8,128)} %fusion.26) | data formatting | bytes 16777216 | tf_op jit(solution)/shard_map/dot_general | solution.py:93
  341.8 9.4 %multiply_reduce_fusion = (f32[128]{0:T(128)S(1)}, bf16[128,2,64,128]{3,2,1,0:T(8,128)(2,1)S(1)}) fusion(f32[128,2,64,128]{3,2,1,0:T(8,128)} %copy.21, f32[128,64]{1,0:T(8,128)S(1)} %copy.19, s32[128,128]{1,0:T(8,128)S(1)} %add_select_fusion, bf16[128,1,64,128]{3,2,1,0:T(8,128)(2,1)} %get-tuple-element.8, bf16[128,1,64,128]{3,2,1,0:T(8,128)(2,1)S(1)} %get-tuple-element.7), kind=kOutput, calls=%fused_computation.4 | convolution fusion | flops 557842304 | bytes 16876032 | tf_op jit(solution)/shard_map/pskb,pab->pska/dot_general | solution.py:34
  351.3 6.7 %convolution_convert_fusion = bf16[256,16384]{1,0:T(8,128)(2,1)} fusion(bf16[16,8,128,128]{3,2,1,0:T(8,128)(2,1)S(1)} %bitcast.60, s32[128]{0:T(128)S(1)} %add_add_fusion), kind=kOutput, calls=%fused_computation | convolution fusion | flops 1077968896 | bytes 12583424 | tf_op jit(solution)/shard_map/dot_general | solution.py:77
  357.9 0.0 all-to-all-done
  357.9 7.3 %all-to-all-start.2 = ((bf16[16,16,16384]{2,1,0:T(8,128)(2,1)}), bf16[16,16,16384]{2,1,0:T(8,128)(2,1)}, u32[]{:S(2)}, u32[]{:S(2)}) async-start(bf16[16,16,16384]{2,1,0:T(8,128)(2,1)} %bitcast.57), calls=%async_computation.2 | async-start | bytes 16777216 | tf_op jit(solution)/shard_map/all_to_all | solution.py:101
  365.2 0.0 all-reduce.4.cloned.1.call-start
  365.3 0.1 sub.32
  365.4 132.5 %all-to-all-done.2 = bf16[16,16,16384]{2,1,0:T(8,128)(2,1)} async-done(((bf16[16,16,16384]{2,1,0:T(8,128)(2,1)}), bf16[16,16,16384]{2,1,0:T(8,128)(2,1)}, u32[]{:S(2)}, u32[]{:S(2)}) %all-to-all-start.2) | async-done | bytes 8388640 | tf_op jit(solution)/shard_map/all_to_all | solution.py:101
  497.9 6.3 %fusion.40 = f32[32,16384]{1,0:T(8,128)} fusion(bf16[256,16384]{1,0:T(8,128)(2,1)} %bitcast.11, s32[256]{0:T(256)S(1)} %sub.32), kind=kOutput, calls=%fused_computation.58 | convolution fusion | flops 268443648 | bytes 10486784 | tf_op jit(solution)/shard_map/dot_general | solution.py:44
  504.2 0.0 all-reduce.4.cloned.1.call-update
  504.2 0.1 convolution_convert_fusion.2
  504.3 0.1 copy.22
  504.5 0.7 reshape.215
  505.2 9.2 %all-to-all-start.3 = ((bf16[16,2,512]{2,1,0:T(2,128)(2,1)}), bf16[16,2,512]{2,1,0:T(2,128)(2,1)S(1)}, u32[]{:S(2)}, u32[]{:S(2)}) async-start(bf16[16,2,512]{2,1,0:T(2,128)(2,1)} %reshape.215), calls=%async_computation.3 | async-start | bytes 65536 | tf_op jit(solution)/shard_map/all_to_all | solution.py:102
  514.4 0.0 copy-done.7
  514.4 0.6 dynamic-slice
  515.7 6.4 %all-to-all-done.3 = bf16[16,2,512]{2,1,0:T(2,128)(2,1)S(1)} async-done(((bf16[16,2,512]{2,1,0:T(2,128)(2,1)}), bf16[16,2,512]{2,1,0:T(2,128)(2,1)S(1)}, u32[]{:S(2)}, u32[]{:S(2)}) %all-to-all-start.3) | async-done | bytes 32800 | tf_op jit(solution)/shard_map/all_to_all | solution.py:102
  522.0 0.1 reshape.216
  522.2 0.2 fusion.39
  522.3 28.4 %all-reduce.1 = f32[32,64]{1,0:T(8,128)S(1)} all-reduce(f32[32,64]{1,0:T(8,128)S(1)} %fusion.39), channel_id=3, replica_groups=mesh['dom'=16,'cls'=8] {'cls'}, use_global_device_ids=true, to_apply=%region_3.4.clone | all-reduce | flops 2048 | bytes 16384
  550.8 0.5 broadcast_multiply_fusion
  551.3 27.6 %all-reduce.4.cloned.1.call-done = f32[32,16384]{1,0:T(8,128)} async-done(((f32[32,16384]{1,0:T(8,128)}), f32[32,16384]{1,0:T(8,128)}) %all-reduce.4.cloned.1.call-update) | async-done | bytes 2097168
  578.9 1.1 dynamic-slice_bitcast_fusion
  580.0 1.0 multiply_add_fusion
  (21 shorter events, 0.2 us)
Async XLA Ops:
  14.4 11.7 %copy-start.5 = (s32[128]{0:T(128)S(1)}, s32[128]{0:T(128)}, u32[]{:S(2)}) copy-start(s32[128]{0:T(128)} %param.10) | copy-start | bytes 1540
  14.5 13.0 %copy-start.2 = (bf16[128,64]{0,1:T(8,128)(2,1)S(1)}, bf16[128,64]{0,1:T(8,128)(2,1)}, u32[]{:S(2)}) copy-start(bf16[128,64]{0,1:T(8,128)(2,1)} %param.13) | copy-start | bytes 49156
  14.5 13.1 %copy-start.4 = (s32[128]{0:T(128)S(1)}, s32[128]{0:T(128)}, u32[]{:S(2)}) copy-start(s32[128]{0:T(128)} %param.9) | copy-start | bytes 1540
  14.5 241.2 %all-to-all-start.1 = ((bf16[128,4,2,64,128]{4,3,2,1,0:T(8,128)(2,1)}), bf16[128,4,2,64,128]{4,3,2,1,0:T(8,128)(2,1)}, u32[]{:S(2)}, u32[]{:S(2)}) async-start(bf16[128,4,2,64,128]{4,3,2,1,0:T(8,128)(2,1)} %stack.6), calls=%async_computation.1 | async-start | bytes 33554432 | tf_op jit(solution)/shard_map/all_to_all | solution.py:83
  36.4 1.3 copy-start.6
  36.4 1.3 copy-start.3
  255.7 102.3 %all-to-all-start = ((bf16[16,1,16]{2,1,0:T(2,128)(2,1)}), bf16[16,1,16]{2,1,0:T(2,128)(2,1)S(1)}, u32[]{:S(2)}, u32[]{:S(2)}) async-start(bf16[16,1,16]{2,1,0:T(2,128)(2,1)} %all_to_all.20), calls=%async_computation | async-start | bytes 16384 | tf_op jit(solution)/shard_map/all_to_all | solution.py:103
  357.9 139.9 %all-to-all-start.2 = ((bf16[16,16,16384]{2,1,0:T(8,128)(2,1)}), bf16[16,16,16384]{2,1,0:T(8,128)(2,1)}, u32[]{:S(2)}, u32[]{:S(2)}) async-start(bf16[16,16,16384]{2,1,0:T(8,128)(2,1)} %bitcast.57), calls=%async_computation.2 | async-start | bytes 16777216 | tf_op jit(solution)/shard_map/all_to_all | solution.py:101
  365.2 213.6 %all-reduce.4.cloned.1.call-start = ((), (), s32[]{:S(2)}) async-start(), calls=%async_computation.4 | async-start | bytes 4194304
  497.9 16.5 %copy-start.7 = (u32[128]{0:T(128)S(1)}, u32[128]{0:T(128)}, u32[]{:S(2)}) copy-start(u32[128]{0:T(128)} %constant.71) | copy-start | bytes 1540
  497.9 82.1 %copy-start = (f32[4,2,64,128]{3,2,1,0:T(8,128)S(1)}, f32[4,2,64,128]{3,2,1,0:T(8,128)}, u32[]{:S(2)}) copy-start(f32[4,2,64,128]{3,2,1,0:T(8,128)} %param.14) | copy-start | bytes 786436
  497.9 82.1 %copy-start.1 = (f32[4,2,64,128]{3,2,1,0:T(8,128)S(1)}, f32[4,2,64,128]{3,2,1,0:T(8,128)}, u32[]{:S(2)}) copy-start(f32[4,2,64,128]{3,2,1,0:T(8,128)} %param.15) | copy-start | bytes 786436
  505.2 16.8 %all-to-all-start.3 = ((bf16[16,2,512]{2,1,0:T(2,128)(2,1)}), bf16[16,2,512]{2,1,0:T(2,128)(2,1)S(1)}, u32[]{:S(2)}, u32[]{:S(2)}) async-start(bf16[16,2,512]{2,1,0:T(2,128)(2,1)} %reshape.215), calls=%async_computation.3 | async-start | bytes 65536 | tf_op jit(solution)/shard_map/all_to_all | solution.py:102
Sparse Core Ops, SparseCore 0:
  504.3 74.4 all-reduce.3
